TPU v7x, 256 devices: a whole 4x4x8 slice. The times are simulated.
256 devices in a mesh: group: 8 (over z_hi, core), shard: 32 (over z_lo, y, x).
Axes of the slice: x: 4, y: 4, z: 8 (z_hi: 4, z_lo: 2; z = z_hi * 2 + z_lo), core: 2. Of those that a mesh axis runs over, the one named last changes fastest.
Arguments:
- latents: bfloat16 [512, 32, 32, 320], P(('group', 'shard')), may hold values from -6 to 6
- cotangent: bfloat16 [512, 32, 32, 320], P(('group', 'shard')), may hold values from -6 to 6
- weights: float32 [8, 2880, 320], P('group', 'shard'), may hold values from -0.109375 to 0.109375
- momentum: float32 [8, 2880, 320], P('group', 'shard'), may hold values from -6 to 6
- step: int32 [1], replicated, may hold values from 0 to 63
Outputs:
- activations: float32 [512, 32, 32, 320], P(('group', 'shard'))
- data_grad: float32 [512, 32, 32, 320], P(('group', 'shard'))
- new_weights: float32 [8, 2880, 320], P('group', 'shard')
- new_momentum: float32 [8, 2880, 320], P('group', 'shard')
Inputs may be any that keep to these rules, and one draw needn't show every extreme that they name: `step`: one value shared by all devices.
All inputs are finite; a program needn't handle non-finite values.
Results may differ from a plain program's by a relative error of at most 0.0029.
Values may be sent and summed in bfloat16 or wider, within the bound.
No kernel may reach another device: no remote copies, remote signals or barrier semaphores. Data moves between devices by JAX's collectives and lax.ppermute only.
A program may use at most 128 MiB of HBM per device.

v0:
```python
from functools import partial
import jax
import jax.numpy as jnp
from jax import lax
from jax.sharding import PartitionSpec as P

beta_rate = 0.9
peak_rate = 0.1
warm_steps = 64.0
tap_offsets = [(row_off, col_off) for row_off in (-1, 0, 1) for col_off in (-1, 0, 1)]


def from_partner(value, axis, bit):
    mask = 2**bit
    pairs = [(source, source ^ mask) for source in range(lax.axis_size(axis))]
    return lax.ppermute(value, axis, pairs)


def shifted_view(padded, row_off, col_off):
    height = padded.shape[1] - 2
    width = padded.shape[2] - 2
    return padded[:, 1 + row_off : 1 + row_off + height, 1 + col_off : 1 + col_off + width, :]


def conv_step(latents, cotangent, kernel):
    channels = kernel.shape[1]
    image_shape = latents.shape
    cell_count = image_shape[0] * image_shape[1] * image_shape[2]
    pad_in = jnp.pad(latents, ((0, 0), (1, 1), (1, 1), (0, 0)))
    pad_co = jnp.pad(cotangent, ((0, 0), (1, 1), (1, 1), (0, 0)))
    flat_co = cotangent.reshape(cell_count, channels)
    forward = jnp.zeros((cell_count, channels), jnp.float32)
    backward = jnp.zeros((cell_count, channels), jnp.float32)
    tap_grads = []
    for tap_index, (row_off, col_off) in enumerate(tap_offsets):
        tap_kernel = kernel[tap_index * channels : (tap_index + 1) * channels]
        moved_in = shifted_view(pad_in, row_off, col_off).reshape(cell_count, channels)
        moved_co = shifted_view(pad_co, -row_off, -col_off).reshape(cell_count, channels)
        forward = forward + jnp.dot(moved_in, tap_kernel, preferred_element_type=jnp.float32)
        backward = backward + lax.dot_general(
            moved_co, tap_kernel, (((1,), (1,)), ((), ())), preferred_element_type=jnp.float32
        )
        tap_grads.append(
            lax.dot_general(
                moved_in, flat_co, (((0,), (0,)), ((), ())), preferred_element_type=jnp.float32
            )
        )
    return (
        forward.reshape(image_shape),
        backward.reshape(image_shape),
        jnp.concatenate(tap_grads, 0),
    )


def trade_pair(payload, level):
    return from_partner(payload, "group", level)


def shards(latents, cotangent, weights, momentum, step):
    kernel_rows = weights[0].astype(jnp.bfloat16)
    kernel = lax.all_gather(kernel_rows, "shard", axis=0, tiled=True)
    forward, backward, partial_grad = conv_step(latents, cotangent, kernel)
    cells_group = lax.axis_size("shard") * latents.shape[0] * latents.shape[1] * latents.shape[2]
    grad_scale = float(cells_group) ** (-0.5)
    learn_rate = peak_rate * (step[0] + 1).astype(jnp.float32) / warm_steps
    shard_rows = weights.shape[1]
    summed = lax.psum(partial_grad, "shard")
    own_rows = lax.dynamic_slice_in_dim(summed, lax.axis_index("shard") * shard_rows, shard_rows, 0)
    moment_new = beta_rate * momentum[0] + own_rows * grad_scale
    updated = weights[0] - learn_rate * moment_new
    bit_count = lax.axis_size("group").bit_length() - 1
    branches = [partial(trade_pair, level=level_index) for level_index in range(bit_count)]
    partner_weights, partner_moment = lax.switch(
        step[0] % bit_count, branches, (updated, moment_new)
    )
    new_weights = (0.5 * (updated + partner_weights))[None]
    new_momentum = (0.5 * (moment_new + partner_moment))[None]
    return (forward, backward, new_weights, new_momentum)


def solution(mesh):
    placed = (
        P(("group", "shard"), None, None, None),
        P(("group", "shard"), None, None, None),
        P("group", "shard", None),
        P("group", "shard", None),
        P(),
    )
    return jax.shard_map(
        shards,
        mesh=mesh,
        in_specs=placed,
        out_specs=(
            P(("group", "shard"), None, None, None),
            P(("group", "shard"), None, None, None),
            P("group", "shard", None),
            P("group", "shard", None),
        ),
        check_vma=False,
    )
```

profile of v0, /device:TPU:32, one launch (start us, length us, event | category | flops | bytes accessed | tf_op | source)
XLA Modules:
  0.0 524.0 jit_solution(8767009696373970491)
XLA Ops:
  7.2 1.0 copy.38
  9.1 3.7 convolution_bitcast_fusion
  12.8 1.7 convolution_bitcast_fusion.1
  14.5 1.7 convolution_bitcast_fusion.2
  16.2 1.7 convolution_bitcast_fusion.3
  17.9 1.7 convolution_bitcast_fusion.5
  19.6 1.7 convolution_bitcast_fusion.6
  21.3 1.7 convolution_bitcast_fusion.7
  23.0 1.7 convolution_bitcast_fusion.8
  24.6 1.7 convolution_bitcast_fusion.4
  26.3 5.0 concatenate.3
  31.3 6.4 %pad_slice_fusion = (bf16[2,32,32,320]{3,2,1,0:T(8,128)(2,1)}, bf16[2,32,32,320]{3,2,1,0:T(8,128)(2,1)}, bf16[2,32,32,320]{3,2,1,0:T(8,128)(2,1)}, bf16[2,32,32,...) fusion(bf16[2,32,32,320]{3,2,1,0:T(8,128)(2,1)S(1)} %copy-done), kind=kLoop, calls=%fused_computation.16 | loop fusion | bytes 11796480 | tf_op jit(solution)/shard_map/slice | solution.py:22
  37.7 6.5 %pad_slice_fusion.8 = (bf16[2,32,32,320]{3,2,1,0:T(8,128)(2,1)}, bf16[2,32,32,320]{3,2,1,0:T(8,128)(2,1)}, bf16[2,32,32,320]{3,2,1,0:T(8,128)(2,1)}, bf16[2,32,3...) fusion(bf16[2,32,32,320]{3,2,1,0:T(8,128)(2,1)S(1)} %copy-done.2), kind=kLoop, calls=%fused_computation.24 | loop fusion | bytes 11796480 | tf_op jit(solution)/shard_map/slice | solution.py:22
  45.1 122.4 %all-gather.3.cloned.1.call-done = bf16[32,90,320]{2,1,0:T(8,128)(2,1)} async-done(((bf16[1,90,320]{2,1,0:T(8,128)(2,1)}), bf16[32,90,320]{2,1,0:T(8,128)(2,1)}) %all-gather.3.cloned.1.call-update) | async-done | bytes 1843216 | tf_op jit(solution)/shard_map/all_gather | solution.py:61
  167.5 2.9 reshape.109
  170.4 2.4 fusion.18
  172.8 0.9 convolution_add_fusion.7
  174.2 0.9 convolution_add_fusion.6
  175.6 0.9 convolution_add_fusion.5
  179.9 0.9 convolution_add_fusion.2
  181.3 0.9 convolution_add_fusion.1
  182.7 2.4 convolution_add_fusion
  185.1 3.4 copy.42
  188.5 2.4 fusion.16
  200.9 2.5 convolution_add_fusion.8
  203.3 3.5 copy.41
  206.8 290.9 %all-reduce.4.cloned.1.call-done = f32[2880,320]{0,1:T(8,128)} async-done(((f32[2880,320]{0,1:T(8,128)}), f32[2880,320]{0,1:T(8,128)}) %all-reduce.4.cloned.1.call-update) | async-done | bytes 3686416 | tf_op jit(solution)/shard_map/psum | solution.py:67
  497.7 1.1 bitcast_subtract_fusion
  498.8 16.8 %conditional.1 = (f32[90,320]{0,1:T(8,128)S(1)}, f32[90,320]{0,1:T(8,128)S(1)}) conditional(s32[]{:T(128)} %clamp.3, (f32[90,320]{0,1:T(8,128)S(1)}, f32[90,320]{0,1:T(8,128)S(1)}) %bitcast_subtract_fusion, (f32[90,320]{0,1:T(8,128)S(1)}, f32[90,320]{0,1:T(8,128)S(1)}) %bitcast_subtract_fusion, (f32[90,320]{0,1:T(8,128)S(1)}, ...), branch_computations={%region_1.2_spmd, %region_2.3_spmd, %region_3.4_spmd} | conditional | bytes 1843296 | solution.py:73
  499.0 5.6 %collective-permute-start.4 = (f32[90,320]{1,0:T(8,128)S(1)}, f32[90,320]{1,0:T(8,128)S(1)}, u32[]{:S(2)}, u32[]{:S(2)}) collective-permute-start(f32[90,320]{1,0:T(8,128)S(1)} %copy.48), channel_id=1, source_target_pairs={{0,128},{32,160},{64,192},{96,224},{128,0},{160,32},{192,64},{224,... | collective-permute-start | bytes 345608 | tf_op jit(solution)/shard_map/cond/branch_2_fun/ppermute | solution.py:16
  505.2 4.6 collective-permute-done.4
  510.0 5.5 %collective-permute-done.5 = f32[90,320]{1,0:T(8,128)S(1)} collective-permute-done((f32[90,320]{1,0:T(8,128)S(1)}, f32[90,320]{1,0:T(8,128)S(1)}, u32[]{:S(2)}, u32[]{:S(2)}) %collective-permute-start.5) | collective-permute-done | bytes 115232 | tf_op jit(solution)/shard_map/cond/branch_2_fun/ppermute | solution.py:16
  (62 shorter events, 18.7 us)
Async XLA Ops:
  7.2 160.3 %all-gather.3.cloned.1.call-start = ((), (), s32[]{:S(2)}) async-start(), calls=%async_computation.1 | async-start | bytes 2433024 | tf_op jit(solution)/shard_map/all_gather | solution.py:61
  9.0 3.8 copy-start
  9.1 3.8 copy-start.2
  9.1 488.7 %all-reduce.4.cloned.1.call-start = ((), (), s32[]{:S(2)}) async-start(), calls=%async_computation | async-start | bytes 7536640 | tf_op jit(solution)/shard_map/psum | solution.py:67
  37.7 7.2 %copy-start.18 = (f32[1,90,320]{2,0,1:T(1,128)S(1)}, f32[1,90,320]{2,0,1:T(1,128)}, u32[]{:S(2)}) copy-start(f32[1,90,320]{2,0,1:T(1,128)} %param.11) | copy-start | bytes 345604
  170.4 2.4 copy-start.17
  172.8 1.4 copy-start.16
  174.2 1.4 copy-start.15
  175.6 1.4 copy-start.1
  177.0 1.4 copy-start.14
  178.4 1.4 copy-start.13
  179.9 1.4 copy-start.12
  181.3 1.4 copy-start.11
  188.5 2.4 copy-start.10
  191.0 1.4 copy-start.9
  192.4 1.4 copy-start.8
  193.8 1.4 copy-start.3
  195.2 1.4 copy-start.7
  196.6 1.4 copy-start.6
  198.0 1.4 copy-start.5
  199.4 1.4 copy-start.4
  499.0 10.9 %collective-permute-start.4 = (f32[90,320]{1,0:T(8,128)S(1)}, f32[90,320]{1,0:T(8,128)S(1)}, u32[]{:S(2)}, u32[]{:S(2)}) collective-permute-start(f32[90,320]{1,0:T(8,128)S(1)} %copy.48), channel_id=1, source_target_pairs={{0,128},{32,160},{64,192},{96,224},{128,0},{160,32},{192,64},{224,... | collective-permute-start | bytes 345608 | tf_op jit(solution)/shard_map/cond/branch_2_fun/ppermute | solution.py:16
  504.7 10.7 %collective-permute-start.5 = (f32[90,320]{1,0:T(8,128)S(1)}, f32[90,320]{1,0:T(8,128)S(1)}, u32[]{:S(2)}, u32[]{:S(2)}) collective-permute-start(f32[90,320]{1,0:T(8,128)S(1)} %copy.49), channel_id=1, source_target_pairs={{0,128},{32,160},{64,192},{96,224},{128,0},{160,32},{192,64},{224,... | collective-permute-start | bytes 345608 | tf_op jit(solution)/shard_map/cond/branch_2_fun/ppermute | solution.py:16
Sparse Core Ops, SparseCore 0:
  10.3 157.0 all-gather.2
  170.1 327.5 all-reduce.3
where the time goes:
time: 525 us; the launch traced here: 524 us
  waiting for transfers between devices  423 us (81%)
  matrix products  39.5 us (8%)
  local copies, waits for them, and re-layouts  38.7 us (7%)
  between operations  15 us (3%)
  starting transfers between devices  6.17 us (1%)
    psum x1, waiting for transfers between devices, shards(): summed = lax.psum(partial_grad, 'shard')  291 us
    all_gather x1, waiting for transfers between devices, shards(): kernel = lax.all_gather(kernel_rows, 'shard', axis=0, tiled=True)  122 us
    dot_general x9, matrix products, conv_step(): lax.dot_general(moved_in, flat_co, (((0,), (0,)), ((), ())), preferred_el...  17.2 us
    unnamed x44, local copies, waits for them, and re-layouts  13.4 us
    slice x2, local copies, waits for them, and re-layouts, shifted_view(): padded[:, 1 + row_off:1 + row_off + height, 1 + col_off:1 + col_off + wid...  12.9 us
    dot_general x9, matrix products, conv_step(): jnp.dot(moved_in, tap_kernel, preferred_element_type=jnp.float32)  11.2 us
    dot_general x9, matrix products, conv_step(): lax.dot_general(moved_co, tap_kernel, (((1,), (1,)), ((), ())), preferred...  11.1 us
  transfers between devices with their start and end apart: 4, of which 4 were waited for; matrix products, arithmetic and copies ran while one was open for 13% of the time, Pallas kernels for 0%

commit v1 on v0

--- a/solution.py
+++ b/solution.py
@@ -8,6 +8,11 @@
 peak_rate = 0.1
 warm_steps = 64.0
 tap_offsets = [(row_off, col_off) for row_off in (-1, 0, 1) for col_off in (-1, 0, 1)]
+
+
+def all_by_exchange(x, name, along):
+    stack = jnp.stack([x] * lax.axis_size(name))
+    return jnp.concatenate(lax.all_to_all(stack, name, 0, 0), axis=along)
 
 
 def from_partner(value, axis, bit):
@@ -58,7 +63,7 @@
 
 def shards(latents, cotangent, weights, momentum, step):
     kernel_rows = weights[0].astype(jnp.bfloat16)
-    kernel = lax.all_gather(kernel_rows, "shard", axis=0, tiled=True)
+    kernel = all_by_exchange(kernel_rows, "shard", 0)
     forward, backward, partial_grad = conv_step(latents, cotangent, kernel)
     cells_group = lax.axis_size("shard") * latents.shape[0] * latents.shape[1] * latents.shape[2]
     grad_scale = float(cells_group) ** (-0.5)

time: 525 us -> 393 us (0.75)
  waiting for transfers between devices: 423 us -> 285 us
  starting transfers between devices: 6.17 us -> 14.9 us
    all_gather x1 -> x0, waiting for transfers between devices: 122 us -> none  [shards(): kernel = lax.all_gather(kernel_rows, 'shard', axis=0, tiled=True)]
    psum x1, waiting for transfers between devices: 291 us -> 275 us  [shards(): summed = lax.psum(partial_grad, 'shard')]
    all_to_all x0 -> x1, starting transfers between devices: none -> 8.73 us  [all_by_exchange(): return jnp.concatenate(lax.all_to_all(stack, name, 0, 0), axis=along)]
    unnamed x44 -> x47, local copies, waits for them, and re-layouts: 13.4 us -> 9.08 us
  transfers between devices with their start and end apart: 4 -> 4, of which waited for: 4 -> 3; matrix products, arithmetic and copies ran while one was open for 13% -> 16% of each run, Pallas kernels for 0% -> 0%
where the time goes in v1:
time: 393 us; the launch traced here: 392 us
  waiting for transfers between devices  285 us (73%)
  local copies, waits for them, and re-layouts  38.6 us (10%)
  matrix products  36.7 us (9%)
  between operations  15.1 us (4%)
  starting transfers between devices  14.9 us (4%)
    psum x1, waiting for transfers between devices, shards(): summed = lax.psum(partial_grad, 'shard')  275 us
    dot_general x9, matrix products, conv_step(): lax.dot_general(moved_in, flat_co, (((0,), (0,)), ((), ())), preferred_el...  14.4 us
    slice x2, local copies, waits for them, and re-layouts, shifted_view(): padded[:, 1 + row_off:1 + row_off + height, 1 + col_off:1 + col_off + wid...  12.9 us
    dot_general x9, matrix products, conv_step(): jnp.dot(moved_in, tap_kernel, preferred_element_type=jnp.float32)  11.2 us
    dot_general x9, matrix products, conv_step(): lax.dot_general(moved_co, tap_kernel, (((1,), (1,)), ((), ())), preferred...  11.1 us
    ppermute x2, waiting for transfers between devices, from_partner(): return lax.ppermute(value, axis, pairs)  10.1 us
    unnamed x47, local copies, waits for them, and re-layouts  9.08 us
    all_to_all x1, starting transfers between devices, all_by_exchange(): return jnp.concatenate(lax.all_to_all(stack, name, 0, 0), axis=along)  8.73 us
  transfers between devices with their start and end apart: 4, of which 3 were waited for; matrix products, arithmetic and copies ran while one was open for 16% of the time, Pallas kernels for 0%

profile of v1, /device:TPU:32, one launch (start us, length us, event | category | flops | bytes accessed | tf_op | source)
XLA Modules:
  0.0 392.1 jit_solution(2774440474400075464)
XLA Ops:
  7.2 1.0 convert_element_type.11
  8.2 1.6 stack.5
  9.8 8.7 %all-to-all-start = ((bf16[32,90,320]{2,1,0:T(8,128)(2,1)}), bf16[32,90,320]{2,1,0:T(8,128)(2,1)}, u32[]{:S(2)}, u32[]{:S(2)}) async-start(bf16[32,90,320]{2,1,0:T(8,128)(2,1)} %stack.5), calls=%async_computation | async-start | bytes 4718592 | tf_op jit(solution)/shard_map/all_to_all | solution.py:15
  18.6 2.4 convolution_bitcast_fusion
  22.8 1.7 convolution_bitcast_fusion.3
  24.5 1.7 convolution_bitcast_fusion.5
  26.3 1.7 convolution_bitcast_fusion.6
  28.0 1.7 convolution_bitcast_fusion.7
  29.7 1.7 convolution_bitcast_fusion.8
  31.3 1.7 convolution_bitcast_fusion.4
  33.0 4.7 %concatenate.3 = f32[2880,320]{0,1:T(8,128)} concatenate(f32[320,320]{0,1:T(8,128)} %convolution_bitcast_fusion.8, f32[320,320]{0,1:T(8,128)} %convolution_bitcast_fusion.7, f32[320,320]{0,1:T(8,128)} %convolution_bitcast_fusion.6, f32[320,320]{0,1:T(8,128)} %convolution_bitcast_fusion.5, f32[320,320]{0,1:T(8,128)} %convolution_bitcast_fusion.4, ...), dimensions={0} | concatenate | bytes 7372800 | tf_op jit(solution)/shard_map/concatenate | solution.py:56
  39.0 6.4 %pad_slice_fusion = (bf16[2,32,32,320]{3,2,1,0:T(8,128)(2,1)}, bf16[2,32,32,320]{3,2,1,0:T(8,128)(2,1)}, bf16[2,32,32,320]{3,2,1,0:T(8,128)(2,1)}, bf16[2,32,32,...) fusion(bf16[2,32,32,320]{3,2,1,0:T(8,128)(2,1)S(1)} %copy-done), kind=kLoop, calls=%fused_computation.16 | loop fusion | bytes 11796480 | tf_op jit(solution)/shard_map/slice | solution.py:27
  45.4 6.5 %pad_slice_fusion.8 = (bf16[2,32,32,320]{3,2,1,0:T(8,128)(2,1)}, bf16[2,32,32,320]{3,2,1,0:T(8,128)(2,1)}, bf16[2,32,32,320]{3,2,1,0:T(8,128)(2,1)}, bf16[2,32,3...) fusion(bf16[2,32,32,320]{3,2,1,0:T(8,128)(2,1)S(1)} %copy-done.3), kind=kLoop, calls=%fused_computation.24 | loop fusion | bytes 11796480 | tf_op jit(solution)/shard_map/slice | solution.py:27
  51.9 2.9 reshape.112
  54.8 2.4 fusion.18
  57.3 0.9 convolution_add_fusion.7
  58.7 0.9 convolution_add_fusion.6
  61.5 0.9 convolution_add_fusion.4
  62.9 0.9 convolution_add_fusion.3
  64.3 0.9 convolution_add_fusion.2
  65.7 0.9 convolution_add_fusion.1
  67.1 2.4 convolution_add_fusion
  69.5 3.4 copy.40
  73.0 2.4 fusion.16
  85.3 2.5 convolution_add_fusion.8
  87.8 3.5 copy.39
  91.3 274.5 %all-reduce.4.cloned.1.call-done = f32[2880,320]{0,1:T(8,128)} async-done(((f32[2880,320]{0,1:T(8,128)}), f32[2880,320]{0,1:T(8,128)}) %all-reduce.4.cloned.1.call-update) | async-done | bytes 3686416 | tf_op jit(solution)/shard_map/psum | solution.py:72
  365.8 1.1 bitcast_subtract_fusion
  366.9 16.8 %conditional.1 = (f32[90,320]{0,1:T(8,128)S(1)}, f32[90,320]{0,1:T(8,128)S(1)}) conditional(s32[]{:T(128)} %clamp.3, (f32[90,320]{0,1:T(8,128)S(1)}, f32[90,320]{0,1:T(8,128)S(1)}) %bitcast_subtract_fusion, (f32[90,320]{0,1:T(8,128)S(1)}, f32[90,320]{0,1:T(8,128)S(1)}) %bitcast_subtract_fusion, (f32[90,320]{0,1:T(8,128)S(1)}, ...), branch_computations={%region_1.2_spmd, %region_2.3_spmd, %region_3.4_spmd} | conditional | bytes 1843296 | solution.py:78
  367.1 5.6 %collective-permute-start.4 = (f32[90,320]{1,0:T(8,128)S(1)}, f32[90,320]{1,0:T(8,128)S(1)}, u32[]{:S(2)}, u32[]{:S(2)}) collective-permute-start(f32[90,320]{1,0:T(8,128)S(1)} %copy.47), channel_id=1, source_target_pairs={{0,128},{32,160},{64,192},{96,224},{128,0},{160,32},{192,64},{224,... | collective-permute-start | bytes 345608 | tf_op jit(solution)/shard_map/cond/branch_2_fun/ppermute | solution.py:21
  373.3 4.6 %collective-permute-done.4 = f32[90,320]{1,0:T(8,128)S(1)} collective-permute-done((f32[90,320]{1,0:T(8,128)S(1)}, f32[90,320]{1,0:T(8,128)S(1)}, u32[]{:S(2)}, u32[]{:S(2)}) %collective-permute-start.4) | collective-permute-done | bytes 115232 | tf_op jit(solution)/shard_map/cond/branch_2_fun/ppermute | solution.py:21
  378.0 5.5 %collective-permute-done.5 = f32[90,320]{1,0:T(8,128)S(1)} collective-permute-done((f32[90,320]{1,0:T(8,128)S(1)}, f32[90,320]{1,0:T(8,128)S(1)}, u32[]{:S(2)}, u32[]{:S(2)}) %collective-permute-start.5) | collective-permute-done | bytes 115232 | tf_op jit(solution)/shard_map/cond/branch_2_fun/ppermute | solution.py:21
  (66 shorter events, 19.2 us)
Async XLA Ops:
  9.8 8.8 %copy-start = (bf16[2,32,32,320]{3,2,1,0:T(8,128)(2,1)S(1)}, bf16[2,32,32,320]{3,2,1,0:T(8,128)(2,1)}, u32[]{:S(2)}) copy-start(bf16[2,32,32,320]{3,2,1,0:T(8,128)(2,1)} %param.9) | copy-start | bytes 3932164
  9.8 42.1 %all-to-all-start = ((bf16[32,90,320]{2,1,0:T(8,128)(2,1)}), bf16[32,90,320]{2,1,0:T(8,128)(2,1)}, u32[]{:S(2)}, u32[]{:S(2)}) async-start(bf16[32,90,320]{2,1,0:T(8,128)(2,1)} %stack.5), calls=%async_computation | async-start | bytes 4718592 | tf_op jit(solution)/shard_map/all_to_all | solution.py:15
  18.5 347.3 %all-reduce.4.cloned.1.call-start = ((), (), s32[]{:S(2)}) async-start(), calls=%async_computation.1 | async-start | bytes 7536640 | tf_op jit(solution)/shard_map/psum | solution.py:72
  18.6 2.4 copy-start.2
  37.7 0.9 copy-start.19
  37.7 1.1 copy-start.20
  39.0 6.4 %copy-start.3 = (bf16[2,32,32,320]{3,2,1,0:T(8,128)(2,1)S(1)}, bf16[2,32,32,320]{3,2,1,0:T(8,128)(2,1)}, u32[]{:S(2)}) copy-start(bf16[2,32,32,320]{3,2,1,0:T(8,128)(2,1)} %param.8) | copy-start | bytes 3932164
  54.8 2.4 copy-start.18
  57.2 1.4 copy-start.17
  58.7 1.4 copy-start.16
  60.1 1.4 copy-start.1
  61.5 1.4 copy-start.15
  62.9 1.4 copy-start.14
  64.3 1.4 copy-start.13
  65.7 1.4 copy-start.12
  73.0 2.4 copy-start.11
  75.4 1.4 copy-start.10
  76.8 1.4 copy-start.9
  78.2 1.4 copy-start.4
  79.7 1.4 copy-start.8
  81.1 1.4 copy-start.7
  82.5 1.4 copy-start.6
  83.9 1.4 copy-start.5
  367.1 10.9 %collective-permute-start.4 = (f32[90,320]{1,0:T(8,128)S(1)}, f32[90,320]{1,0:T(8,128)S(1)}, u32[]{:S(2)}, u32[]{:S(2)}) collective-permute-start(f32[90,320]{1,0:T(8,128)S(1)} %copy.47), channel_id=1, source_target_pairs={{0,128},{32,160},{64,192},{96,224},{128,0},{160,32},{192,64},{224,... | collective-permute-start | bytes 345608 | tf_op jit(solution)/shard_map/cond/branch_2_fun/ppermute | solution.py:21
  372.8 10.7 %collective-permute-start.5 = (f32[90,320]{1,0:T(8,128)S(1)}, f32[90,320]{1,0:T(8,128)S(1)}, u32[]{:S(2)}, u32[]{:S(2)}) collective-permute-start(f32[90,320]{1,0:T(8,128)S(1)} %copy.48), channel_id=1, source_target_pairs={{0,128},{32,160},{64,192},{96,224},{128,0},{160,32},{192,64},{224,... | collective-permute-start | bytes 345608 | tf_op jit(solution)/shard_map/cond/branch_2_fun/ppermute | solution.py:21
Sparse Core Ops, SparseCore 0:
  37.9 327.8 all-reduce.3
